TPU v7x, 512 devices: a whole 4x8x8 slice. The times are simulated.
512 devices in a mesh: row: 64 (over z, x, core), col: 8 (over y).
Axes of the slice: x: 4, y: 8, z: 8, core: 2. Of those that a mesh axis runs over, the one named last changes fastest.
Arguments:
- amplitudes: bfloat16 [512, 256, 256], P('col', 'row'), may hold values from -6 to 6
- integrals: bfloat16 [256, 48, 256, 256], P('row', 'col'), may hold values from -0.03125 to 0.03125
- screen: int32 [256, 48], P('row', 'col'), may hold values from -1 to 7, as said below
- owner_map: int32 [8, 8], P('col'), may hold values from 0 to 7, each once within a row
Outputs:
- ladder: float32 [512, 64, 256], P('row', 'col')
Inputs may be any that keep to these rules, and one draw needn't show every extreme that they name: `screen`: in each row and column group the 6 slots first name distinct result tiles of that group, then hold -1; at least 2 are live, and some group of some row has all 6 live.
All inputs are finite; a program needn't handle non-finite values.
Results may differ from a plain program's by a relative error of at most 0.0003.
Values may be sent and summed in bfloat16 or wider, within the bound.
A program may use at most 64 MiB of HBM per device.

v0:
```python
import jax
import jax.numpy as jnp
from jax import lax
from jax.sharding import PartitionSpec as P


def body(amplitudes, integrals, screen, owner_map):
    gathered = lax.all_gather(amplitudes, "col", axis=0, tiled=True)
    group_tiles = owner_map.shape[1]
    live_slot = screen >= 0
    labels = jnp.arange(group_tiles, dtype=jnp.int32)
    matches = screen[:, :, None] == labels[None, None, :]
    stored = jnp.sum(jnp.where(matches, owner_map[0][None, None, :], 0), axis=2)
    selector = ((stored[:, :, None] == labels[None, None, :]) & live_slot[:, :, None]).astype(
        jnp.bfloat16
    )
    placed = jnp.einsum(
        "kla,klwv->kawv", selector, integrals, preferred_element_type=jnp.float32
    ).astype(jnp.bfloat16)
    return lax.psum_scatter(
        jnp.einsum("pkw,kawv->pav", gathered, placed, preferred_element_type=jnp.float32),
        "row",
        scatter_dimension=0,
        tiled=True,
    )


def solution(mesh):
    return jax.shard_map(
        body,
        mesh=mesh,
        in_specs=(
            P("col", "row", None),
            P("row", "col", None, None),
            P("row", "col"),
            P("col", None),
        ),
        out_specs=P("row", "col", None),
        check_vma=False,
    )
```

profile of v0, /device:TPU:8, one launch (start us, length us, event | category | flops | bytes accessed | tf_op | source)
XLA Modules:
  0.0 226.7 jit_solution(1776103147567017797)
XLA Ops:
  6.5 0.0 copy-start
  6.5 0.0 all-gather.2.cloned.1.call-start
  6.5 1.7 copy.12
  8.2 0.0 all-gather.2.cloned.1.call-update
  8.3 0.0 reduce-scatter.2.cloned.1.call-start
  8.3 0.8 copy.9
  9.1 0.9 select_reduce_fusion
  10.0 0.1 copy.10
  10.1 0.7 broadcast_compare_fusion
  10.8 0.0 copy-done
  10.8 3.9 %fusion.4 = bf16[4,8,256,256]{3,1,2,0:T(8,128)(2,1)} fusion(bf16[4,6,256,256]{3,2,1,0:T(8,128)(2,1)S(1)} %copy-done, s32[4,6]{1,0:T(4,128)S(1)} %copy.10, pred[4,6]{1,0:T(4,128)(4,1)S(1)} %broadcast_compare_fusion), kind=kOutput, calls=%fused_computation.4 | convolution fusion | flops 27263360 | bytes 7340152 | tf_op jit(solution)/shard_map/kla,klwv->kawv/dot_general | solution.py:17
  14.7 39.9 %all-gather.2.cloned.1.call-done = bf16[512,4,256]{2,0,1:T(8,128)(2,1)} async-done(((bf16[64,4,256]{2,0,1:T(8,128)(2,1)}), bf16[512,4,256]{2,0,1:T(8,128)(2,1)}) %all-gather.2.cloned.1.call-update) | async-done | bytes 1048592 | tf_op jit(solution)/shard_map/all_gather | solution.py:8
  54.6 7.1 %fusion.7 = f32[512,8,256]{0,2,1:T(8,128)} fusion(bf16[4,8,256,256]{3,1,2,0:T(8,128)(2,1)} %fusion.4, bf16[512,4,256]{2,0,1:T(8,128)(2,1)} %all-gather.2.cloned.1.call-done), kind=kOutput, calls=%fused_computation.5 | convolution fusion | flops 2147483648 | bytes 9437184 | tf_op jit(solution)/shard_map/pkw,kawv->pav/dot_general | solution.py:21
  61.7 5.4 %copy.14 = f32[512,8,256]{2,1,0:T(8,128)} copy(f32[512,8,256]{0,2,1:T(8,128)} %fusion.7) | data formatting | bytes 8388608 | tf_op jit(solution)/shard_map/pkw,kawv->pav/dot_general | solution.py:21
  67.2 0.0 reduce-scatter.2.cloned.1.call-update
  67.2 152.7 %reduce-scatter.2.cloned.1.call-done = f32[8,8,256]{2,1,0:T(8,128)} async-done(((f32[512,8,256]{2,1,0:T(8,128)}), f32[8,8,256]{2,1,0:T(8,128)}) %reduce-scatter.2.cloned.1.call-update) | async-done | bytes 65552 | tf_op jit(solution)/shard_map/reduce_scatter | solution.py:20
Async XLA Ops:
  6.5 4.2 %copy-start = (bf16[4,6,256,256]{3,2,1,0:T(8,128)(2,1)S(1)}, bf16[4,6,256,256]{3,2,1,0:T(8,128)(2,1)}, u32[]{:S(2)}) copy-start(bf16[4,6,256,256]{3,2,1,0:T(8,128)(2,1)} %param.5) | copy-start | bytes 9437188
  6.5 48.1 %all-gather.2.cloned.1.call-start = ((), (), s32[]{:S(2)}) async-start(), calls=%async_computation.1 | async-start | bytes 1179648 | tf_op jit(solution)/shard_map/all_gather | solution.py:8
  8.3 211.6 %reduce-scatter.2.cloned.1.call-start = ((), (), s32[]{:S(2)}) async-start(), calls=%async_computation.2 | async-start | bytes 4259840 | tf_op jit(solution)/shard_map/reduce_scatter | solution.py:20
Sparse Core Ops, SparseCore 0:
  9.4 45.1 all-gather.1
  67.3 152.4 reduce-scatter.1
where the time goes:
time: 227 us
  waiting for transfers between devices  193 us (85%)
  between operations  13.4 us (6%)
  matrix products  11.1 us (5%)
  local copies, waits for them, and re-layouts  8.01 us (4%)
    reduce_scatter x1, waiting for transfers between devices, body(): lax.psum_scatter(jnp.einsum('pkw,kawv->pav', gathered, placed, preferred_...  153 us
    all_gather x1, waiting for transfers between devices, body(): gathered = lax.all_gather(amplitudes, 'col', axis=0, tiled=True)  39.9 us
    dot_general x1, matrix products, body(): jnp.einsum('pkw,kawv->pav', gathered, placed, preferred_element_type=jnp....  7.13 us
    dot_general x1, local copies, waits for them, and re-layouts, body(): jnp.einsum('pkw,kawv->pav', gathered, placed, preferred_element_type=jnp....  5.44 us
  transfers between devices with their start and end apart: 2, of which 2 were waited for; matrix products, arithmetic and copies ran while one was open for 3% of the time, Pallas kernels for 0%

commit v1 on v0

v1 whole, which is shorter than its diff:
```python
import functools

import jax
import jax.numpy as jnp
from jax import lax
from jax.experimental import pallas as pl
from jax.experimental.pallas import tpu as pltpu
from jax.sharding import PartitionSpec as P

MESH = pl.DeviceIdType.MESH
NX, NZ, NY = 4, 8, 8


def kernel(screen_ref, owner_ref, amp_ref, integrals_ref, out_ref,
           tiles, pick, gath, part, mate, fromx, red, fromz,
           load_sem, y_send, y_recv, c_send, c_recv, x_send, x_recv, z_send, z_recv):
    row, y = lax.axis_index("row"), lax.axis_index("col")
    core = lax.rem(row, 2)
    x = lax.rem(row // 2, NX)
    z = row // (2 * NX)

    def dev(zz, xx, cc):
        return ((zz * NX + xx) * 2 + cc, y)

    right = (row, lax.rem(y + 1, NY))
    left = (row, lax.rem(y + NY - 1, NY))

    load = pltpu.make_async_copy(integrals_ref, tiles.at[pl.ds(0, 24)], load_sem)
    load.start()

    barrier = pltpu.get_barrier_semaphore()
    peers = [right, left, dev(z, x, 1 - core)]
    peers += [dev(z, lax.rem(x + o, NX), core) for o in range(1, NX)]
    peers += [dev(lax.rem(z + o, NZ), x, core) for o in range(1, NZ)]
    for peer in peers:
        pl.semaphore_signal(barrier, inc=1, device_id=peer, device_id_type=MESH)
    pl.semaphore_wait(barrier, len(peers))

    def y_copy(step, d):
        src = amp_ref if step == 1 else gath.at[step - 1, :, d]
        return pltpu.make_async_remote_copy(
            src_ref=src, dst_ref=gath.at[step, :, d],
            send_sem=y_send.at[step, d], recv_sem=y_recv.at[step, d],
            device_id=right if d == 0 else left, device_id_type=MESH)

    def c_copy(slot):
        return pltpu.make_async_remote_copy(
            src_ref=part.at[slot, 1 - core], dst_ref=mate.at[slot],
            send_sem=c_send.at[slot], recv_sem=c_recv.at[slot],
            device_id=dev(z, x, 1 - core), device_id_type=MESH)

    def x_copy(slot, o):
        xx = lax.rem(x + o, NX)
        return pltpu.make_async_remote_copy(
            src_ref=part.at[slot, core, xx], dst_ref=fromx.at[slot, o - 1],
            send_sem=x_send.at[slot, o - 1], recv_sem=x_recv.at[slot, o - 1],
            device_id=dev(z, xx, core), device_id_type=MESH)

    def block_of(slot):
        if slot == 0:
            return y
        s = (slot + 1) // 2
        return lax.rem(y + NY - s, NY) if slot % 2 == 1 else lax.rem(y + s, NY)

    def z_copy(slot):
        return pltpu.make_async_remote_copy(
            src_ref=red.at[slot], dst_ref=fromz.at[z],
            send_sem=z_send.at[slot], recv_sem=z_recv.at[z],
            device_id=dev(block_of(slot), x, core), device_id_type=MESH)

    y_copy(1, 0).start()
    y_copy(1, 1).start()

    tiles[24] = jnp.zeros((256, 256), jnp.bfloat16)
    for t in range(8):
        label = jnp.int32(0)
        for g in range(8):
            label = jnp.where(owner_ref[0, g] == t, g, label)
        for k in range(4):
            at = jnp.int32(24)
            for l in range(6):
                at = jnp.where(screen_ref[k, l] == label, k * 6 + l, at)
            pick[k * 8 + t] = at
    load.wait()

    def product(step):
        single = step == 0 or step == 4
        slots = [0] if step == 0 else ([7] if step == 4 else [2 * step - 1, 2 * step])

        def tile(t, carry):
            total = None
            for k in range(4):
                if step == 0:
                    rows = amp_ref[k]
                elif step == 4:
                    rows = gath[4, k, 0]
                else:
                    rows = gath[step, k].reshape(128, 256)
                term = jnp.dot(rows, tiles[pick[k * 8 + t]], preferred_element_type=jnp.float32)
                total = term if total is None else total + term
            total = total.reshape(len(slots), NX, 2, 8, 256)
            for i, slot in enumerate(slots):
                for xx in range(NX):
                    for cc in range(2):
                        part[slot, cc, xx, t] = total[i, xx, cc]
            return carry

        lax.fori_loop(0, 8, tile, 0)
        for slot in slots:
            c_copy(slot).start()
        return slots

    def join(slots):
        for slot in slots:
            c_copy(slot).wait()

            def add(xx, carry):
                part[slot, core, xx] = part[slot, core, xx] + mate[slot, xx]
                return carry

            lax.fori_loop(0, NX, add, 0)
            for o in (2, 1, 3):
                x_copy(slot, o).start()

    def across(slots):
        for slot in slots:
            for o in range(1, NX):
                x_copy(slot, o).wait()
            total = part[slot, core, x]
            for o in range(1, NX):
                total = total + fromx[slot, o - 1]
            block = block_of(slot)

            @pl.when(block == z)
            def _():
                fromz[z] = total

            @pl.when(block != z)
            def _():
                red[slot] = total
                z_copy(slot).start()

    done = []
    for step in range(5):
        if step >= 1:
            for d in range(2):
                if d == 1 and step == 4:
                    continue
                y_copy(step, d).wait()
                if step + 1 <= 4 - d:
                    y_copy(step + 1, d).start()
        done.append(product(step))
        if step >= 1:
            join(done[step - 1])
        if step >= 2:
            across(done[step - 2])
    join(done[4])
    across(done[3])
    across(done[4])

    for slot in range(8):
        @pl.when(block_of(slot) != z)
        def _():
            z_copy(slot).wait_send()

    total = fromz[z]
    for o in range(1, NZ):
        zz = lax.rem(z + o, NZ)
        pltpu.make_async_remote_copy(
            src_ref=red.at[0], dst_ref=fromz.at[zz],
            send_sem=z_send.at[0], recv_sem=z_recv.at[zz],
            device_id=dev(zz, x, core), device_id_type=MESH).wait_recv()
        total = total + fromz[zz]
    out_ref[...] = total


def body(amplitudes, integrals, screen, owner_map):
    amp = jnp.transpose(amplitudes, (1, 0, 2))
    tiles = integrals.reshape(24, 256, 256)
    f32 = jnp.float32
    dma = pltpu.SemaphoreType.DMA
    out = pl.pallas_call(
        kernel,
        out_shape=jax.ShapeDtypeStruct((8, 8, 256), f32),
        in_specs=[
            pl.BlockSpec(memory_space=pltpu.SMEM),
            pl.BlockSpec(memory_space=pltpu.SMEM),
            pl.BlockSpec(memory_space=pltpu.VMEM),
            pl.BlockSpec(memory_space=pl.ANY),
        ],
        out_specs=pl.BlockSpec(memory_space=pltpu.VMEM),
        scratch_shapes=[
            pltpu.VMEM((25, 256, 256), jnp.bfloat16),
            pltpu.SMEM((32,), jnp.int32),
            pltpu.VMEM((5, 4, 2, 64, 256), jnp.bfloat16),
            pltpu.VMEM((8, 2, NX, 8, 8, 256), f32),
            pltpu.VMEM((8, NX, 8, 8, 256), f32),
            pltpu.VMEM((8, NX - 1, 8, 8, 256), f32),
            pltpu.VMEM((8, 8, 8, 256), f32),
            pltpu.VMEM((8, 8, 8, 256), f32),
            dma(()),
            dma((5, 2)), dma((5, 2)),
            dma((8,)), dma((8,)),
            dma((8, 3)), dma((8, 3)),
            dma((8,)), dma((8,)),
        ],
        compiler_params=pltpu.CompilerParams(collective_id=0, has_side_effects=True),
    )(screen, owner_map, amp, tiles)
    return jnp.transpose(out, (1, 0, 2))


def solution(mesh):
    return jax.shard_map(
        body,
        mesh=mesh,
        in_specs=(
            P("col", "row", None),
            P("row", "col", None, None),
            P("row", "col"),
            P("col", None),
        ),
        out_specs=P("row", "col", None),
        check_vma=False,
    )
```

time: 227 us -> 56.5 us (0.25)
  the two profiles are of different devices: /device:TPU:8 before, /device:TPU:40 now
where the time goes in v1:
time: 56.5 us; the launch traced here: 56.3 us
  Pallas kernels  53.3 us (94%)
  local copies, waits for them, and re-layouts  3.05 us (5%)
    pallas_call x1, Pallas kernels, body(): pl.pallas_call(kernel, out_shape=jax.ShapeDtypeStruct((8, 8, 256), f32),...  53.3 us
    unnamed x1, local copies, waits for them, and re-layouts  1.56 us
    transpose x1, local copies, waits for them, and re-layouts, body(): return jnp.transpose(out, (1, 0, 2))  1.49 us

profile of v1, /device:TPU:40, one launch (start us, length us, event | category | flops | bytes accessed | tf_op | source)
XLA Modules:
  0.0 56.3 jit_solution(11627548489584165209)
XLA Ops:
  0.0 1.6 %copy.8 = bf16[64,4,256]{2,0,1:T(8,128)(2,1)} copy(bf16[64,4,256]{2,1,0:T(4,128)(2,1)} %param.4) | data formatting | bytes 262144 | tf_op args[0]
  1.6 53.3 %shard_map.46 = f32[8,8,256]{2,1,0:T(8,128)} custom-call(s32[4,6]{1,0:T(4,128)} %screen_ref.1, s32[1,8]{1,0:T(1,128)} %owner_ref.1, bf16[4,64,256]{2,1,0:T(8,128)(2,1)} %bitcast.6, bf16[24,256,256]{2,1,0:T(8,128)(2,1)} %bitcast.5), custom_call_target="tpu_custom_call" | custom-call | tf_op jit(solution)/shard_map/pallas_call | solution.py:182
  54.8 1.5 %copy.6 = f32[8,8,256]{2,1,0:T(8,128)} copy(f32[8,8,256]{2,0,1:T(8,128)} %bitcast.7) | data formatting | bytes 131072 | tf_op jit(solution)/shard_map/transpose | solution.py:209

commit v2 on v1

v2 whole, which is shorter than its diff:
```python
import jax
import jax.numpy as jnp
from jax import lax
from jax.experimental import pallas as pl
from jax.experimental.pallas import tpu as pltpu
from jax.sharding import PartitionSpec as P

MESH = pl.DeviceIdType.MESH
NX, NZ, NY = 4, 8, 8


def kernel(screen_ref, owner_ref, amp_ref, integrals_ref, out_ref,
           tiles, pick, gath, part, mate, relay, near, red, fromz, last,
           load_sem, y_send, y_recv, c_send, c_recv, x_send, x_recv, z_send, z_recv, l_send, l_recv):
    row, y = lax.axis_index("row"), lax.axis_index("col")
    core = lax.rem(row, 2)
    x = lax.rem(row // 2, NX)
    z = row // (2 * NX)

    def dev(zz, xx, cc):
        return ((zz * NX + xx) * 2 + cc, y)

    right = (row, lax.rem(y + 1, NY))
    left = (row, lax.rem(y + NY - 1, NY))
    xp, xf, xm = (lax.rem(x + o, NX) for o in (1, 2, 3))
    zp, zm = lax.rem(z + 1, NZ), lax.rem(z + NZ - 1, NZ)

    load = pltpu.make_async_copy(integrals_ref, tiles.at[pl.ds(0, 24)], load_sem)
    load.start()

    barrier = pltpu.get_barrier_semaphore()
    peers = [right, left, dev(z, x, 1 - core), dev(z, xp, core), dev(z, xm, core)]
    peers += [dev(lax.rem(z + o, NZ), x, core) for o in range(1, NZ)]
    for peer in peers:
        pl.semaphore_signal(barrier, inc=1, device_id=peer, device_id_type=MESH)
    pl.semaphore_wait(barrier, len(peers))

    def y_copy(step, d, h):
        k = pl.ds(2 * h, 2)
        src = amp_ref.at[k] if step == 1 else gath.at[step - 1, k, d]
        return pltpu.make_async_remote_copy(
            src_ref=src, dst_ref=gath.at[step, k, d],
            send_sem=y_send.at[step, d, h], recv_sem=y_recv.at[step, d, h],
            device_id=right if d == 0 else left, device_id_type=MESH)

    def c_copy(slot):
        return pltpu.make_async_remote_copy(
            src_ref=part.at[slot, 1 - core], dst_ref=mate.at[slot],
            send_sem=c_send.at[slot], recv_sem=c_recv.at[slot],
            device_id=dev(z, x, 1 - core), device_id_type=MESH)

    low, high = pl.ds(0, 4), pl.ds(4, 4)

    def x_copy(slot, i):
        to = xp if i % 2 == 0 else xm
        half = low if i in (0, 3, 4) else high
        piece = xf if i < 2 else to
        dst = relay.at[slot, i] if i < 2 else near.at[slot, i % 2, half]
        return pltpu.make_async_remote_copy(
            src_ref=part.at[slot, core, piece, half], dst_ref=dst,
            send_sem=x_send.at[slot, i], recv_sem=x_recv.at[slot, i],
            device_id=dev(z, to, core), device_id_type=MESH)

    def block_of(slot):
        if slot == 0:
            return y
        s = (slot + 1) // 2
        return lax.rem(y + NY - s, NY) if slot % 2 == 1 else lax.rem(y + s, NY)

    def ahead(slot):
        return lax.rem(block_of(slot) + NZ - z, NZ)

    def z_copy(slot, d, half):
        return pltpu.make_async_remote_copy(
            src_ref=red.at[slot, half], dst_ref=fromz.at[slot, d, half],
            send_sem=z_send.at[slot, d], recv_sem=z_recv.at[slot, d],
            device_id=dev(zp if d == 0 else zm, x, core), device_id_type=MESH)

    whole = pl.ds(0, 8)

    def last_copy(at):
        return pltpu.make_async_remote_copy(
            src_ref=red.at[7], dst_ref=last.at[at],
            send_sem=l_send, recv_sem=l_recv.at[at],
            device_id=dev(block_of(7), x, core), device_id_type=MESH)

    for h in range(2):
        for d in range(2):
            y_copy(1, d, h).start()

    tiles[24] = jnp.zeros((256, 256), jnp.bfloat16)
    for t in range(8):
        label = jnp.int32(0)
        for g in range(8):
            label = jnp.where(owner_ref[0, g] == t, g, label)
        for k in range(4):
            at = jnp.int32(24)
            for l in range(6):
                at = jnp.where(screen_ref[k, l] == label, k * 6 + l, at)
            pick[k * 8 + t] = at
    load.wait()

    groups = [[0], [1, 2], [3, 4], [5, 6], [7]]

    def gather(step):
        for h in range(2):
            for d in range(2):
                if step == 4 and d != h:
                    continue
                y_copy(step, d, h).wait()
                if step < 3 or (step == 3 and d == h):
                    y_copy(step + 1, d, h).start()

    def product(step):
        slots = groups[step]

        def tile(t, carry):
            total = None
            for k in range(4):
                if step == 0:
                    rows = amp_ref[k]
                elif step == 4:
                    rows = gath[4, k, k // 2]
                else:
                    rows = gath[step, k].reshape(128, 256)
                term = jnp.dot(rows, tiles[pick[k * 8 + t]], preferred_element_type=jnp.float32)
                total = term if total is None else total + term
            total = total.reshape(len(slots), NX, 2, 8, 256)
            for i, slot in enumerate(slots):
                for xx in range(NX):
                    for cc in range(2):
                        part[slot, cc, xx, t] = total[i, xx, cc]
            return carry

        lax.fori_loop(0, 8, tile, 0)
        for slot in slots:
            c_copy(slot).start()

    def join(step):
        for slot in groups[step]:
            c_copy(slot).wait()

            def add(o, carry):
                xx = lax.rem(x + o, NX)
                part[slot, core, xx] = part[slot, core, xx] + mate[slot, xx]
                return carry

            lax.fori_loop(0, NX, add, 0)
            for i in range(4):
                x_copy(slot, i).start()

    def pass_on(step):
        for slot in groups[step]:
            for i, to, half in ((0, xp, low), (1, xm, high)):
                x_copy(slot, i).wait()
                part[slot, core, to, half] = part[slot, core, to, half] + relay[slot, i]
                x_copy(slot, 4 + i).start()

    def across(step):
        for slot in groups[step]:
            for i in range(2, 6):
                x_copy(slot, i).wait()
            red[slot] = part[slot, core, x] + near[slot, 0] + near[slot, 1]
            if slot < 7:
                @pl.when(ahead(slot) == 4)
                def _():
                    z_copy(slot, 0, low).start()
                    z_copy(slot, 1, high).start()
            else:
                @pl.when(ahead(slot) != 0)
                def _():
                    last_copy(ahead(slot) - 1).start()

    def hop(step, n):
        for slot in groups[step]:
            for d, at, first in ((0, 5 - n, low), (1, 3 + n, high)):
                half = first if n == 2 else whole

                @pl.when(ahead(slot) == at)
                def _():
                    z_copy(slot, d, half).wait_recv()
                    red[slot, half] = red[slot, half] + fromz[slot, d, half]
                    z_copy(slot, d, whole).start()

    product(0)
    gather(1)
    join(0)
    product(1)
    pass_on(0)
    gather(2)
    join(1)
    across(0)
    product(2)
    pass_on(1)
    hop(0, 2)
    gather(3)
    join(2)
    across(1)
    hop(0, 3)
    product(3)
    pass_on(2)
    hop(1, 2)
    hop(0, 4)
    gather(4)
    join(3)
    across(2)
    hop(1, 3)
    product(4)
    pass_on(3)
    hop(2, 2)
    hop(1, 4)
    join(4)
    across(3)
    hop(2, 3)
    pass_on(4)
    hop(3, 2)
    hop(2, 4)
    across(4)
    hop(3, 3)
    hop(3, 4)

    for slot in range(7):
        p = ahead(slot)

        @pl.when(p == 0)
        def _():
            z_copy(slot, 0, whole).wait_recv()
            z_copy(slot, 1, whole).wait_recv()
            out_ref[...] = red[slot] + fromz[slot, 0] + fromz[slot, 1]

        @pl.when(p == 4)
        def _():
            z_copy(slot, 0, low).wait_send()
            z_copy(slot, 1, high).wait_send()

        @pl.when((p > 0) & (p < 4))
        def _():
            z_copy(slot, 0, whole).wait_send()

        @pl.when(p > 4)
        def _():
            z_copy(slot, 1, whole).wait_send()

    @pl.when(ahead(7) == 0)
    def _():
        total = red[7]
        for o in range(7):
            last_copy(o).wait_recv()
            total = total + last[o]
        out_ref[...] = total

    @pl.when(ahead(7) != 0)
    def _():
        last_copy(ahead(7) - 1).wait_send()


def body(amplitudes, integrals, screen, owner_map):
    amp = jnp.transpose(amplitudes, (1, 0, 2))
    tiles = integrals.reshape(24, 256, 256)
    f32 = jnp.float32
    dma = pltpu.SemaphoreType.DMA
    out = pl.pallas_call(
        kernel,
        out_shape=jax.ShapeDtypeStruct((8, 8, 256), f32),
        in_specs=[
            pl.BlockSpec(memory_space=pltpu.SMEM),
            pl.BlockSpec(memory_space=pltpu.SMEM),
            pl.BlockSpec(memory_space=pltpu.VMEM),
            pl.BlockSpec(memory_space=pl.ANY),
        ],
        out_specs=pl.BlockSpec(memory_space=pltpu.VMEM),
        scratch_shapes=[
            pltpu.VMEM((25, 256, 256), jnp.bfloat16),
            pltpu.SMEM((32,), jnp.int32),
            pltpu.VMEM((5, 4, 2, 64, 256), jnp.bfloat16),
            pltpu.VMEM((8, 2, NX, 8, 8, 256), f32),
            pltpu.VMEM((8, NX, 8, 8, 256), f32),
            pltpu.VMEM((8, 2, 4, 8, 256), f32),
            pltpu.VMEM((8, 2, 8, 8, 256), f32),
            pltpu.VMEM((8, 8, 8, 256), f32),
            pltpu.VMEM((7, 2, 8, 8, 256), f32),
            pltpu.VMEM((7, 8, 8, 256), f32),
            dma(()),
            dma((5, 2, 2)), dma((5, 2, 2)),
            dma((8,)), dma((8,)),
            dma((8, 6)), dma((8, 6)),
            dma((7, 2)), dma((7, 2)),
            dma(()), dma((7,)),
        ],
        compiler_params=pltpu.CompilerParams(collective_id=0, has_side_effects=True),
    )(screen, owner_map, amp, tiles)
    return jnp.transpose(out, (1, 0, 2))


def solution(mesh):
    return jax.shard_map(
        body,
        mesh=mesh,
        in_specs=(
            P("col", "row", None),
            P("row", "col", None, None),
            P("row", "col"),
            P("col", None),
        ),
        out_specs=P("row", "col", None),
        check_vma=False,
    )
```

time: 56.5 us -> 63.3 us (1.12)
  Pallas kernels: 53.3 us -> 60 us
    pallas_call x1, Pallas kernels: 53.3 us -> 60 us  [body(): pl.pallas_call(kernel, out_shape=jax.ShapeDtypeStruct((8, 8, 256), f32),...]
where the time goes in v2:
time: 63.3 us; the launch traced here: 63 us
  Pallas kernels  60 us (95%)
  local copies, waits for them, and re-layouts  3.05 us (5%)
    pallas_call x1, Pallas kernels, body(): pl.pallas_call(kernel, out_shape=jax.ShapeDtypeStruct((8, 8, 256), f32),...  60 us
    unnamed x1, local copies, waits for them, and re-layouts  1.56 us
    transpose x1, local copies, waits for them, and re-layouts, body(): return jnp.transpose(out, (1, 0, 2))  1.49 us

profile of v2, /device:TPU:40, one launch (start us, length us, event | category | flops | bytes accessed | tf_op | source)
XLA Modules:
  0.0 63.0 jit_solution(9877219924498562246)
XLA Ops:
  0.0 1.6 %copy.8 = bf16[64,4,256]{2,0,1:T(8,128)(2,1)} copy(bf16[64,4,256]{2,1,0:T(4,128)(2,1)} %param.4) | data formatting | bytes 262144 | tf_op args[0]
  1.6 60.0 %shard_map.46 = f32[8,8,256]{2,1,0:T(8,128)} custom-call(s32[4,6]{1,0:T(4,128)} %screen_ref.1, s32[1,8]{1,0:T(1,128)} %owner_ref.1, bf16[4,64,256]{2,1,0:T(8,128)(2,1)} %bitcast.6, bf16[24,256,256]{2,1,0:T(8,128)(2,1)} %bitcast.5), custom_call_target="tpu_custom_call" | custom-call | tf_op jit(solution)/shard_map/pallas_call | solution.py:262
  61.6 1.5 %copy.6 = f32[8,8,256]{2,1,0:T(8,128)} copy(f32[8,8,256]{2,0,1:T(8,128)} %bitcast.7) | data formatting | bytes 131072 | tf_op jit(solution)/shard_map/transpose | solution.py:292

commit v3 on v1

v3 whole, which is shorter than its diff:
```python
import jax
import jax.numpy as jnp
from jax import lax
from jax.experimental import pallas as pl
from jax.experimental.pallas import tpu as pltpu
from jax.sharding import PartitionSpec as P

MESH = pl.DeviceIdType.MESH
NX, NZ, NY = 4, 8, 8


def kernel(screen_ref, owner_ref, amp_ref, integrals_ref, out_ref,
           tiles, pick, gath, part, mate, fromx, red, fromz,
           load_sem, y_send, y_recv, c_send, c_recv, x_send, x_recv, z_send, z_recv):
    row, y = lax.axis_index("row"), lax.axis_index("col")
    core = lax.rem(row, 2)
    x = lax.rem(row // 2, NX)
    z = row // (2 * NX)

    def dev(zz, xx, cc):
        return ((zz * NX + xx) * 2 + cc, y)

    right = (row, lax.rem(y + 1, NY))
    left = (row, lax.rem(y + NY - 1, NY))

    load = pltpu.make_async_copy(integrals_ref, tiles.at[pl.ds(0, 24)], load_sem)
    load.start()

    barrier = pltpu.get_barrier_semaphore()
    peers = [right, left, dev(z, x, 1 - core)]
    peers += [dev(z, lax.rem(x + o, NX), core) for o in range(1, NX)]
    peers += [dev(lax.rem(z + o, NZ), x, core) for o in range(1, NZ)]
    for peer in peers:
        pl.semaphore_signal(barrier, inc=1, device_id=peer, device_id_type=MESH)
    pl.semaphore_wait(barrier, len(peers))

    def y_copy(step, d, h):
        k = pl.ds(2 * h, 2)
        src = amp_ref.at[k] if step == 1 else gath.at[step - 1, k, d]
        return pltpu.make_async_remote_copy(
            src_ref=src, dst_ref=gath.at[step, k, d],
            send_sem=y_send.at[step, d, h], recv_sem=y_recv.at[step, d, h],
            device_id=right if d == 0 else left, device_id_type=MESH)

    def pieces(slot):
        return [(slot, pl.ds(0, 8))] if slot < 7 else [(7, pl.ds(0, 4)), (8, pl.ds(4, 4))]

    def c_copy(slot, i, ts):
        return pltpu.make_async_remote_copy(
            src_ref=part.at[slot, 1 - core, :, ts], dst_ref=mate.at[slot, :, ts],
            send_sem=c_send.at[i], recv_sem=c_recv.at[i],
            device_id=dev(z, x, 1 - core), device_id_type=MESH)

    def x_copy(slot, o, i, ts):
        xx = lax.rem(x + o, NX)
        return pltpu.make_async_remote_copy(
            src_ref=part.at[slot, core, xx, ts], dst_ref=fromx.at[slot, o - 1, ts],
            send_sem=x_send.at[i, o - 1], recv_sem=x_recv.at[i, o - 1],
            device_id=dev(z, xx, core), device_id_type=MESH)

    def block_of(slot):
        if slot == 0:
            return y
        s = (slot + 1) // 2
        return lax.rem(y + NY - s, NY) if slot % 2 == 1 else lax.rem(y + s, NY)

    def z_copy(slot, i, ts):
        return pltpu.make_async_remote_copy(
            src_ref=red.at[slot, ts], dst_ref=fromz.at[z, ts],
            send_sem=z_send.at[i], recv_sem=z_recv.at[z, max(i - 7, 0)],
            device_id=dev(block_of(slot), x, core), device_id_type=MESH)

    for h in range(2):
        for d in range(2):
            y_copy(1, d, h).start()

    tiles[24] = jnp.zeros((256, 256), jnp.bfloat16)
    for t in range(8):
        label = jnp.int32(0)
        for g in range(8):
            label = jnp.where(owner_ref[0, g] == t, g, label)
        for k in range(4):
            at = jnp.int32(24)
            for l in range(6):
                at = jnp.where(screen_ref[k, l] == label, k * 6 + l, at)
            pick[k * 8 + t] = at
    load.wait()

    groups = [[0], [1, 2], [3, 4], [5, 6], [7]]

    def gather(step):
        for h in range(2):
            for d in range(2):
                if step == 4 and d != h:
                    continue
                y_copy(step, d, h).wait()
                if step < 3 or (step == 3 and d == h):
                    y_copy(step + 1, d, h).start()

    def product(step):
        slots = groups[step]

        def tile(t, carry):
            total = None
            for k in range(4):
                if step == 0:
                    rows = amp_ref[k]
                elif step == 4:
                    rows = gath[4, k, k // 2]
                else:
                    rows = gath[step, k].reshape(128, 256)
                term = jnp.dot(rows, tiles[pick[k * 8 + t]], preferred_element_type=jnp.float32)
                total = term if total is None else total + term
            total = total.reshape(len(slots), NX, 2, 8, 256)
            for i, slot in enumerate(slots):
                for xx in range(NX):
                    for cc in range(2):
                        part[slot, cc, xx, t] = total[i, xx, cc]
            return carry

        for n in range(len(pieces(slots[-1]))):
            size = 8 // len(pieces(slots[-1]))
            lax.fori_loop(n * size, (n + 1) * size, tile, 0)
            for slot in slots:
                c_copy(slot, *pieces(slot)[n]).start()

    def join(step):
        for slot in groups[step]:
            for i, ts in pieces(slot):
                c_copy(slot, i, ts).wait()
                for o in (2, 1, 3, 0):
                    xx = lax.rem(x + o, NX)
                    part[slot, core, xx, ts] = part[slot, core, xx, ts] + mate[slot, xx, ts]
                    if o:
                        x_copy(slot, o, i, ts).start()

    def across(step):
        for slot in groups[step]:
            block = block_of(slot)
            for i, ts in pieces(slot):
                for o in range(1, NX):
                    x_copy(slot, o, i, ts).wait()
                total = part[slot, core, x, ts]
                for o in range(1, NX):
                    total = total + fromx[slot, o - 1, ts]

                @pl.when(block == z)
                def _():
                    fromz[z, ts] = total

                @pl.when(block != z)
                def _():
                    red[slot, ts] = total
                    z_copy(slot, i, ts).start()

    product(0)
    for step in range(1, 5):
        gather(step)
        product(step)
        join(step - 1)
        if step >= 2:
            across(step - 2)
    join(4)
    across(3)
    across(4)

    for slot in range(8):
        @pl.when(block_of(slot) != z)
        def _():
            for i, ts in pieces(slot):
                z_copy(slot, i, ts).wait_send()

    def arrived(slot):
        for o in range(1, NZ):
            zz = lax.rem(z + o, NZ)
            for i, ts in pieces(slot):
                pltpu.make_async_remote_copy(
                    src_ref=red.at[0, ts], dst_ref=fromz.at[zz, ts],
                    send_sem=z_send.at[0], recv_sem=z_recv.at[zz, max(i - 7, 0)],
                    device_id=dev(zz, x, core), device_id_type=MESH).wait_recv()

    @pl.when(block_of(7) != z)
    def _():
        arrived(0)

    @pl.when(block_of(7) == z)
    def _():
        arrived(7)

    total = fromz[0]
    for zz in range(1, NZ):
        total = total + fromz[zz]
    out_ref[...] = total


def body(amplitudes, integrals, screen, owner_map):
    amp = jnp.transpose(amplitudes, (1, 0, 2))
    tiles = integrals.reshape(24, 256, 256)
    f32 = jnp.float32
    dma = pltpu.SemaphoreType.DMA
    out = pl.pallas_call(
        kernel,
        out_shape=jax.ShapeDtypeStruct((8, 8, 256), f32),
        in_specs=[
            pl.BlockSpec(memory_space=pltpu.SMEM),
            pl.BlockSpec(memory_space=pltpu.SMEM),
            pl.BlockSpec(memory_space=pltpu.VMEM),
            pl.BlockSpec(memory_space=pl.ANY),
        ],
        out_specs=pl.BlockSpec(memory_space=pltpu.VMEM),
        scratch_shapes=[
            pltpu.VMEM((25, 256, 256), jnp.bfloat16),
            pltpu.SMEM((32,), jnp.int32),
            pltpu.VMEM((5, 4, 2, 64, 256), jnp.bfloat16),
            pltpu.VMEM((8, 2, NX, 8, 8, 256), f32),
            pltpu.VMEM((8, NX, 8, 8, 256), f32),
            pltpu.VMEM((8, NX - 1, 8, 8, 256), f32),
            pltpu.VMEM((8, 8, 8, 256), f32),
            pltpu.VMEM((8, 8, 8, 256), f32),
            dma(()),
            dma((5, 2, 2)), dma((5, 2, 2)),
            dma((9,)), dma((9,)),
            dma((9, 3)), dma((9, 3)),
            dma((9,)), dma((8, 2)),
        ],
        compiler_params=pltpu.CompilerParams(collective_id=0, has_side_effects=True),
    )(screen, owner_map, amp, tiles)
    return jnp.transpose(out, (1, 0, 2))


def solution(mesh):
    return jax.shard_map(
        body,
        mesh=mesh,
        in_specs=(
            P("col", "row", None),
            P("row", "col", None, None),
            P("row", "col"),
            P("col", None),
        ),
        out_specs=P("row", "col", None),
        check_vma=False,
    )
```

time: 56.5 us -> 56.3 us (level)
  the two profiles are of different devices: /device:TPU:40 before, /device:TPU:32 now
where the time goes in v3:
time: 56.3 us; the launch traced here: 56.1 us
  Pallas kernels  53 us (94%)
  local copies, waits for them, and re-layouts  3.05 us (5%)
    pallas_call x1, Pallas kernels, body(): pl.pallas_call(kernel, out_shape=jax.ShapeDtypeStruct((8, 8, 256), f32),...  53 us
    unnamed x1, local copies, waits for them, and re-layouts  1.56 us
    transpose x1, local copies, waits for them, and re-layouts, body(): return jnp.transpose(out, (1, 0, 2))  1.49 us

profile of v3, /device:TPU:32, one launch (start us, length us, event | category | flops | bytes accessed | tf_op | source)
XLA Modules:
  0.0 56.1 jit_solution(14688279154556137102)
XLA Ops:
  0.0 1.6 %copy.8 = bf16[64,4,256]{2,0,1:T(8,128)(2,1)} copy(bf16[64,4,256]{2,1,0:T(4,128)(2,1)} %param.4) | data formatting | bytes 262144 | tf_op args[0]
  1.6 53.0 %shard_map.46 = f32[8,8,256]{2,1,0:T(8,128)} custom-call(s32[4,6]{1,0:T(4,128)} %screen_ref.1, s32[1,8]{1,0:T(1,128)} %owner_ref.1, bf16[4,64,256]{2,1,0:T(8,128)(2,1)} %bitcast.6, bf16[24,256,256]{2,1,0:T(8,128)(2,1)} %bitcast.5), custom_call_target="tpu_custom_call" | custom-call | tf_op jit(solution)/shard_map/pallas_call | solution.py:201
  54.6 1.5 %copy.6 = f32[8,8,256]{2,1,0:T(8,128)} copy(f32[8,8,256]{2,0,1:T(8,128)} %bitcast.7) | data formatting | bytes 131072 | tf_op jit(solution)/shard_map/transpose | solution.py:228
